TPU v7x, 256 devices: a whole 4x4x8 slice. The times are simulated.
256 devices in a mesh: seq: 32 (over x_lo, z, core), batch: 8 (over y, x_hi).
Axes of the slice: x: 4 (x_hi: 2, x_lo: 2; x = x_hi * 2 + x_lo), y: 4, z: 8, core: 2. Of those that a mesh axis runs over, the one named last changes fastest.
Arguments:
- queries: bfloat16 [65536, 2048], P(('batch', 'seq')), parts along dimension 0, may hold values from -9 to 9
- key_rows: bfloat16 [65536, 2048], P(('batch', 'seq')), parts along dimension 0, may hold values from -9 to 9
- values: bfloat16 [65536, 2048], P(('batch', 'seq')), parts along dimension 0, may hold values from -6 to 6
- bias_tiles: bfloat16 [3, 256, 256], replicated, may hold values from -6 to 6
- buckets: int32 [5], replicated, may hold values from 0 to 2
- slopes: float32 [32], replicated, may hold values from 0.3 to 1.5
Outputs:
- attended: bfloat16 [65536, 2048], P(('batch', 'seq')), parts along dimension 0
There are 8 independent parts, one for each index of `batch`. A program takes and returns all parts, laid end to end along the dimension named above; an argument that names none is the same for every part. Nothing has to cross between parts.
All inputs are finite; a program needn't handle non-finite values.
Results may differ from a plain program's by a relative error of at most 0.0043.
Values may be sent and summed in bfloat16 or wider, within the bound.
A program may use at most 128 MiB of HBM per device.

v0:
```python
import jax
import jax.numpy as jnp
from jax import lax
from jax.sharding import PartitionSpec as P

HD = 64
WIN = 4


def passed_along(shard, axis, by):
    devices = lax.axis_size(axis)
    return lax.ppermute(shard, axis, [(i, (i + by) % devices) for i in range(devices)])


def window_bias(bias_tiles, buckets):
    pieces = []
    for offset in range(-WIN, WIN + 1):
        tile = bias_tiles[buckets[abs(offset)]].astype(jnp.float32)
        if offset < 0:
            tile = tile.T
        pieces.append(tile)
    return jnp.concatenate(pieces, axis=1)


def block_attention(query_part, key_part, value_part, bias_window, slope_part):
    head_count = slope_part.shape[0]
    head_width = query_part.shape[1] // head_count
    group_size = min(head_count, 4)
    group_count = head_count // group_size
    row_count = query_part.shape[0]
    key_count = key_part.shape[0]
    query_groups = query_part.reshape(row_count, group_count, group_size, head_width).transpose(
        1, 0, 2, 3
    )
    key_groups = key_part.reshape(key_count, group_count, group_size, head_width).transpose(
        1, 0, 2, 3
    )
    value_groups = value_part.reshape(key_count, group_count, group_size, head_width).transpose(
        1, 0, 2, 3
    )
    slope_groups = slope_part.reshape(group_count, group_size)

    def per_group(packed):
        query_one, key_one, value_one, slope_one = packed
        scores = jnp.einsum("qgd,kgd->gqk", query_one, key_one, preferred_element_type=jnp.float32)
        scores = scores * HD ** (-0.5) + slope_one[:, None, None] * bias_window[None]
        peaks = jnp.max(scores, axis=-1, keepdims=True)
        raised = jnp.exp(scores - peaks)
        totals = jnp.sum(raised, axis=-1)
        weights = raised.astype(jnp.bfloat16)
        weighted = jnp.einsum(
            "gqk,kgd->qgd", weights, value_one, preferred_element_type=jnp.float32
        )
        return (weighted / totals.T[:, :, None]).astype(jnp.bfloat16)

    results = lax.map(per_group, (query_groups, key_groups, value_groups, slope_groups))
    return results.transpose(1, 0, 2, 3).reshape(row_count, head_count * head_width)


def per_device(queries, key_rows, values, bias_tiles, buckets, slopes):
    bias_window = window_bias(bias_tiles, buckets)
    paired = jnp.stack((key_rows, values), axis=0)
    above_blocks = []
    below_blocks = []
    upper_pair = paired
    lower_pair = paired
    for step in range(WIN):
        upper_pair = passed_along(upper_pair, "seq", -1)
        above_blocks.append(upper_pair)
        lower_pair = passed_along(lower_pair, "seq", 1)
        below_blocks.append(lower_pair)
    ordered = below_blocks[::-1] + [paired] + above_blocks
    window_pairs = jnp.concatenate(ordered, axis=1)
    return block_attention(queries, window_pairs[0], window_pairs[1], bias_window, slopes)


def solution(mesh):
    in_specs = (
        P(("batch", "seq"), None),
        P(("batch", "seq"), None),
        P(("batch", "seq"), None),
        P(),
        P(),
        P(),
    )
    out_specs = P(("batch", "seq"), None)
    return jax.shard_map(
        per_device, mesh=mesh, in_specs=in_specs, out_specs=out_specs, check_vma=False
    )
```

profile of v0, /device:TPU:8, one launch (start us, length us, event | category | flops | bytes accessed | tf_op | source)
XLA Modules:
  0.0 223.9 jit_solution(16697095501206115676)
XLA Ops:
  0.0 1.8 pad_maximum_fusion
  2.0 6.3 %collective-permute-start.4 = (bf16[2,256,2048]{2,1,0:T(8,128)(2,1)S(1)}, bf16[2,256,2048]{2,1,0:T(8,128)(2,1)S(1)}, u32[]{:S(2)}, u32[]{:S(2)}) collective-permute-start(bf16[2,256,2048]{2,1,0:T(8,128)(2,1)S(1)} %pad_maximum_fusion), channel_id=1, source_target_pairs={{0,248},{8,0},{16,8},{24,16},{32,24},{40,32},{48,40},{56,48},{64,5... | collective-permute-start | bytes 6291464 | tf_op jit(solution)/shard_map/ppermute | solution.py:12
  8.3 23.6 %collective-permute-done = bf16[2,256,2048]{2,1,0:T(8,128)(2,1)S(1)} collective-permute-done((bf16[2,256,2048]{2,1,0:T(8,128)(2,1)S(1)}, bf16[2,256,2048]{2,1,0:T(8,128)(2,1)S(1)}, u32[]{:S(2)}, u32[]{:S(2)}) %collective-permute-start) | collective-permute-done | bytes 2097184 | tf_op jit(solution)/shard_map/ppermute | solution.py:12
  33.2 3.9 %collective-permute-start.5 = (bf16[2,256,2048]{2,1,0:T(8,128)(2,1)S(1)}, bf16[2,256,2048]{2,1,0:T(8,128)(2,1)}, u32[]{:S(2)}, u32[]{:S(2)}) collective-permute-start(bf16[2,256,2048]{2,1,0:T(8,128)(2,1)S(1)} %collective-permute-done.4), channel_id=1, source_target_pairs={{0,248},{8,0},{16,8},{24,16},{32,24},{40,32},{48,40},{56,48},{64,5... | collective-permute-start | bytes 6291464 | tf_op jit(solution)/shard_map/ppermute | solution.py:12
  37.1 22.3 %collective-permute-done.1 = bf16[2,256,2048]{2,1,0:T(8,128)(2,1)S(1)} collective-permute-done((bf16[2,256,2048]{2,1,0:T(8,128)(2,1)S(1)}, bf16[2,256,2048]{2,1,0:T(8,128)(2,1)S(1)}, u32[]{:S(2)}, u32[]{:S(2)}) %collective-permute-start.1) | collective-permute-done | bytes 2097184 | tf_op jit(solution)/shard_map/ppermute | solution.py:12
  60.7 4.1 %collective-permute-start.6 = (bf16[2,256,2048]{2,1,0:T(8,128)(2,1)}, bf16[2,256,2048]{2,1,0:T(8,128)(2,1)}, u32[]{:S(2)}, u32[]{:S(2)}) collective-permute-start(bf16[2,256,2048]{2,1,0:T(8,128)(2,1)} %collective-permute-done.5), channel_id=1, source_target_pairs={{0,248},{8,0},{16,8},{24,16},{32,24},{40,32},{48,40},{56,48},{64,5... | collective-permute-start | bytes 6291464 | tf_op jit(solution)/shard_map/ppermute | solution.py:12
  64.8 22.3 %collective-permute-done.2 = bf16[2,256,2048]{2,1,0:T(8,128)(2,1)} collective-permute-done((bf16[2,256,2048]{2,1,0:T(8,128)(2,1)S(1)}, bf16[2,256,2048]{2,1,0:T(8,128)(2,1)}, u32[]{:S(2)}, u32[]{:S(2)}) %collective-permute-start.2) | collective-permute-done | bytes 2097184 | tf_op jit(solution)/shard_map/ppermute | solution.py:12
  101.4 4.1 %collective-permute-start.7 = (bf16[2,256,2048]{2,1,0:T(8,128)(2,1)}, bf16[2,256,2048]{2,1,0:T(8,128)(2,1)S(1)}, u32[]{:S(2)}, u32[]{:S(2)}) collective-permute-start(bf16[2,256,2048]{2,1,0:T(8,128)(2,1)} %collective-permute-done.6), channel_id=1, source_target_pairs={{0,248},{8,0},{16,8},{24,16},{32,24},{40,32},{48,40},{56,48},{64,5... | collective-permute-start | bytes 6291464 | tf_op jit(solution)/shard_map/ppermute | solution.py:12
  105.5 9.5 %collective-permute-done.3 = bf16[2,256,2048]{2,1,0:T(8,128)(2,1)} collective-permute-done((bf16[2,256,2048]{2,1,0:T(8,128)(2,1)}, bf16[2,256,2048]{2,1,0:T(8,128)(2,1)}, u32[]{:S(2)}, u32[]{:S(2)}) %collective-permute-start.3) | collective-permute-done | bytes 2097184 | tf_op jit(solution)/shard_map/ppermute | solution.py:12
  116.9 2.0 constant_dynamic-update-slice_fusion.7
  123.1 1.8 constant_dynamic-update-slice_fusion.1
  125.0 4.4 %collective-permute-done.7 = bf16[2,256,2048]{2,1,0:T(8,128)(2,1)S(1)} collective-permute-done((bf16[2,256,2048]{2,1,0:T(8,128)(2,1)}, bf16[2,256,2048]{2,1,0:T(8,128)(2,1)S(1)}, u32[]{:S(2)}, u32[]{:S(2)}) %collective-permute-start.7) | collective-permute-done | bytes 2097184 | tf_op jit(solution)/shard_map/ppermute | solution.py:12
  129.6 7.3 %fusion.40 = (bf16[1,2304,2048]{2,1,0:T(8,128)(2,1)}, bf16[1,2304,2048]{2,1,0:T(8,128)(2,1)}) fusion(bf16[2,2304,2048]{2,1,0:T(8,128)(2,1)S(1)} %constant_dynamic-update-slice_fusion), kind=kLoop, calls=%fused_computation.45 | loop fusion | bytes 37748736 | tf_op jit(solution)/shard_map/slice | solution.py:74
  136.9 12.8 %copy.15 = bf16[1,2304,2048]{1,2,0:T(8,128)(2,1)} copy(bf16[1,2304,2048]{2,1,0:T(8,128)(2,1)} %get-tuple-element.60) | data formatting | bytes 18874368 | tf_op jit(solution)/shard_map/slice | solution.py:74
  149.7 12.8 %copy.17 = bf16[1,2304,2048]{1,2,0:T(8,128)(2,1)} copy(bf16[1,2304,2048]{2,1,0:T(8,128)(2,1)} %get-tuple-element.59) | data formatting | bytes 18874368 | tf_op jit(solution)/shard_map/slice | solution.py:74
  162.5 60.0 %while.10 = (s32[]{:T(128)}, bf16[8,256,4,64]{1,3,2,0:T(8,128)(2,1)S(1)}, bf16[8,2304,4,64]{1,3,2,0:T(8,128)(2,1)}, bf16[8,256,4,64]{1,3,2,0:T(8,128)(2,1)}, bf1...) while((s32[]{:T(128)}, ...), condition=%wide.region_3.4_spmd, body=%wide.region_0.3_spmd.sunk | while | flops 622983168 | bytes 33314960 | solution.py:56
  162.5 3.2 %fusion.51 = (f32[4,256]{1,0:T(4,128)S(1)}, f32[4,256,2304]{2,1,0:T(8,128)S(1)}) fusion(f32[256,2304]{1,0:T(8,128)S(1)} %get-tuple-element.139, f32[4]{0:T(128)S(1)} %fusion.50, bf16[8,2304,4,64]{1,3,2,0:T(8,128)(2,1)} %get-tuple-element.137, s32[]{:T(128)S(6)} %copy.42, bf16[8,256,4,64]{1,3,2,0:T(8,128)(2,1)} %get-tuple-element.136), kind=kOutput, calls=%fused_computation.44.clone.1 | convolution fusion | flops 311426048 | bytes 13112336 | tf_op jit(solution)/shard_map/while/body/eval_jaxpr/qgd,kgd->gqk/dot_general | solution.py:45
  167.1 2.9 %fusion.53 = bf16[8,256,4,64]{1,3,2,0:T(8,128)(2,1)S(1)} fusion(bf16[8,256,4,64]{1,3,2,0:T(8,128)(2,1)S(1)} %get-tuple-element.126, s32[]{:T(128)S(6)} %copy.42, f32[4,256,2304]{2,1,0:T(8,128)S(1)} %get-tuple-element.115, f32[4,256]{1,0:T(4,128)S(1)} %get-tuple-element.116, bf16[8,2304,4,64]{1,3,2,0:T(8,128)(2,1)} %get-tuple-element.135, ...), kind=kOutput, calls=%fused_computation.14.clone.1 | convolution fusion | flops 306839552 | bytes 10757120 | tf_op jit(solution)/shard_map/while/body/eval_jaxpr/gqk,kgd->qgd/dot_general | solution.py:51
  170.0 3.2 %fusion.51 = (f32[4,256]{1,0:T(4,128)S(1)}, f32[4,256,2304]{2,1,0:T(8,128)S(1)}) fusion(f32[256,2304]{1,0:T(8,128)S(1)} %get-tuple-element.139, f32[4]{0:T(128)S(1)} %fusion.50, bf16[8,2304,4,64]{1,3,2,0:T(8,128)(2,1)} %get-tuple-element.137, s32[]{:T(128)S(6)} %copy.42, bf16[8,256,4,64]{1,3,2,0:T(8,128)(2,1)} %get-tuple-element.136), kind=kOutput, calls=%fused_computation.44.clone.1 | convolution fusion | flops 311426048 | bytes 13112336 | tf_op jit(solution)/shard_map/while/body/eval_jaxpr/qgd,kgd->gqk/dot_general | solution.py:45
  174.6 2.9 %fusion.53 = bf16[8,256,4,64]{1,3,2,0:T(8,128)(2,1)S(1)} fusion(bf16[8,256,4,64]{1,3,2,0:T(8,128)(2,1)S(1)} %get-tuple-element.126, s32[]{:T(128)S(6)} %copy.42, f32[4,256,2304]{2,1,0:T(8,128)S(1)} %get-tuple-element.115, f32[4,256]{1,0:T(4,128)S(1)} %get-tuple-element.116, bf16[8,2304,4,64]{1,3,2,0:T(8,128)(2,1)} %get-tuple-element.135, ...), kind=kOutput, calls=%fused_computation.14.clone.1 | convolution fusion | flops 306839552 | bytes 10757120 | tf_op jit(solution)/shard_map/while/body/eval_jaxpr/gqk,kgd->qgd/dot_general | solution.py:51
  177.5 3.2 %fusion.51 = (f32[4,256]{1,0:T(4,128)S(1)}, f32[4,256,2304]{2,1,0:T(8,128)S(1)}) fusion(f32[256,2304]{1,0:T(8,128)S(1)} %get-tuple-element.139, f32[4]{0:T(128)S(1)} %fusion.50, bf16[8,2304,4,64]{1,3,2,0:T(8,128)(2,1)} %get-tuple-element.137, s32[]{:T(128)S(6)} %copy.42, bf16[8,256,4,64]{1,3,2,0:T(8,128)(2,1)} %get-tuple-element.136), kind=kOutput, calls=%fused_computation.44.clone.1 | convolution fusion | flops 311426048 | bytes 13112336 | tf_op jit(solution)/shard_map/while/body/eval_jaxpr/qgd,kgd->gqk/dot_general | solution.py:45
  182.1 2.9 %fusion.53 = bf16[8,256,4,64]{1,3,2,0:T(8,128)(2,1)S(1)} fusion(bf16[8,256,4,64]{1,3,2,0:T(8,128)(2,1)S(1)} %get-tuple-element.126, s32[]{:T(128)S(6)} %copy.42, f32[4,256,2304]{2,1,0:T(8,128)S(1)} %get-tuple-element.115, f32[4,256]{1,0:T(4,128)S(1)} %get-tuple-element.116, bf16[8,2304,4,64]{1,3,2,0:T(8,128)(2,1)} %get-tuple-element.135, ...), kind=kOutput, calls=%fused_computation.14.clone.1 | convolution fusion | flops 306839552 | bytes 10757120 | tf_op jit(solution)/shard_map/while/body/eval_jaxpr/gqk,kgd->qgd/dot_general | solution.py:51
  185.0 3.2 %fusion.51 = (f32[4,256]{1,0:T(4,128)S(1)}, f32[4,256,2304]{2,1,0:T(8,128)S(1)}) fusion(f32[256,2304]{1,0:T(8,128)S(1)} %get-tuple-element.139, f32[4]{0:T(128)S(1)} %fusion.50, bf16[8,2304,4,64]{1,3,2,0:T(8,128)(2,1)} %get-tuple-element.137, s32[]{:T(128)S(6)} %copy.42, bf16[8,256,4,64]{1,3,2,0:T(8,128)(2,1)} %get-tuple-element.136), kind=kOutput, calls=%fused_computation.44.clone.1 | convolution fusion | flops 311426048 | bytes 13112336 | tf_op jit(solution)/shard_map/while/body/eval_jaxpr/qgd,kgd->gqk/dot_general | solution.py:45
  189.6 2.9 %fusion.53 = bf16[8,256,4,64]{1,3,2,0:T(8,128)(2,1)S(1)} fusion(bf16[8,256,4,64]{1,3,2,0:T(8,128)(2,1)S(1)} %get-tuple-element.126, s32[]{:T(128)S(6)} %copy.42, f32[4,256,2304]{2,1,0:T(8,128)S(1)} %get-tuple-element.115, f32[4,256]{1,0:T(4,128)S(1)} %get-tuple-element.116, bf16[8,2304,4,64]{1,3,2,0:T(8,128)(2,1)} %get-tuple-element.135, ...), kind=kOutput, calls=%fused_computation.14.clone.1 | convolution fusion | flops 306839552 | bytes 10757120 | tf_op jit(solution)/shard_map/while/body/eval_jaxpr/gqk,kgd->qgd/dot_general | solution.py:51
  192.5 3.2 %fusion.51 = (f32[4,256]{1,0:T(4,128)S(1)}, f32[4,256,2304]{2,1,0:T(8,128)S(1)}) fusion(f32[256,2304]{1,0:T(8,128)S(1)} %get-tuple-element.139, f32[4]{0:T(128)S(1)} %fusion.50, bf16[8,2304,4,64]{1,3,2,0:T(8,128)(2,1)} %get-tuple-element.137, s32[]{:T(128)S(6)} %copy.42, bf16[8,256,4,64]{1,3,2,0:T(8,128)(2,1)} %get-tuple-element.136), kind=kOutput, calls=%fused_computation.44.clone.1 | convolution fusion | flops 311426048 | bytes 13112336 | tf_op jit(solution)/shard_map/while/body/eval_jaxpr/qgd,kgd->gqk/dot_general | solution.py:45
  197.1 2.9 %fusion.53 = bf16[8,256,4,64]{1,3,2,0:T(8,128)(2,1)S(1)} fusion(bf16[8,256,4,64]{1,3,2,0:T(8,128)(2,1)S(1)} %get-tuple-element.126, s32[]{:T(128)S(6)} %copy.42, f32[4,256,2304]{2,1,0:T(8,128)S(1)} %get-tuple-element.115, f32[4,256]{1,0:T(4,128)S(1)} %get-tuple-element.116, bf16[8,2304,4,64]{1,3,2,0:T(8,128)(2,1)} %get-tuple-element.135, ...), kind=kOutput, calls=%fused_computation.14.clone.1 | convolution fusion | flops 306839552 | bytes 10757120 | tf_op jit(solution)/shard_map/while/body/eval_jaxpr/gqk,kgd->qgd/dot_general | solution.py:51
  200.0 3.2 %fusion.51 = (f32[4,256]{1,0:T(4,128)S(1)}, f32[4,256,2304]{2,1,0:T(8,128)S(1)}) fusion(f32[256,2304]{1,0:T(8,128)S(1)} %get-tuple-element.139, f32[4]{0:T(128)S(1)} %fusion.50, bf16[8,2304,4,64]{1,3,2,0:T(8,128)(2,1)} %get-tuple-element.137, s32[]{:T(128)S(6)} %copy.42, bf16[8,256,4,64]{1,3,2,0:T(8,128)(2,1)} %get-tuple-element.136), kind=kOutput, calls=%fused_computation.44.clone.1 | convolution fusion | flops 311426048 | bytes 13112336 | tf_op jit(solution)/shard_map/while/body/eval_jaxpr/qgd,kgd->gqk/dot_general | solution.py:45
  204.6 2.9 %fusion.53 = bf16[8,256,4,64]{1,3,2,0:T(8,128)(2,1)S(1)} fusion(bf16[8,256,4,64]{1,3,2,0:T(8,128)(2,1)S(1)} %get-tuple-element.126, s32[]{:T(128)S(6)} %copy.42, f32[4,256,2304]{2,1,0:T(8,128)S(1)} %get-tuple-element.115, f32[4,256]{1,0:T(4,128)S(1)} %get-tuple-element.116, bf16[8,2304,4,64]{1,3,2,0:T(8,128)(2,1)} %get-tuple-element.135, ...), kind=kOutput, calls=%fused_computation.14.clone.1 | convolution fusion | flops 306839552 | bytes 10757120 | tf_op jit(solution)/shard_map/while/body/eval_jaxpr/gqk,kgd->qgd/dot_general | solution.py:51
  207.5 3.2 %fusion.51 = (f32[4,256]{1,0:T(4,128)S(1)}, f32[4,256,2304]{2,1,0:T(8,128)S(1)}) fusion(f32[256,2304]{1,0:T(8,128)S(1)} %get-tuple-element.139, f32[4]{0:T(128)S(1)} %fusion.50, bf16[8,2304,4,64]{1,3,2,0:T(8,128)(2,1)} %get-tuple-element.137, s32[]{:T(128)S(6)} %copy.42, bf16[8,256,4,64]{1,3,2,0:T(8,128)(2,1)} %get-tuple-element.136), kind=kOutput, calls=%fused_computation.44.clone.1 | convolution fusion | flops 311426048 | bytes 13112336 | tf_op jit(solution)/shard_map/while/body/eval_jaxpr/qgd,kgd->gqk/dot_general | solution.py:45
  212.1 2.9 %fusion.53 = bf16[8,256,4,64]{1,3,2,0:T(8,128)(2,1)S(1)} fusion(bf16[8,256,4,64]{1,3,2,0:T(8,128)(2,1)S(1)} %get-tuple-element.126, s32[]{:T(128)S(6)} %copy.42, f32[4,256,2304]{2,1,0:T(8,128)S(1)} %get-tuple-element.115, f32[4,256]{1,0:T(4,128)S(1)} %get-tuple-element.116, bf16[8,2304,4,64]{1,3,2,0:T(8,128)(2,1)} %get-tuple-element.135, ...), kind=kOutput, calls=%fused_computation.14.clone.1 | convolution fusion | flops 306839552 | bytes 10757120 | tf_op jit(solution)/shard_map/while/body/eval_jaxpr/gqk,kgd->qgd/dot_general | solution.py:51
  215.0 3.2 %fusion.51 = (f32[4,256]{1,0:T(4,128)S(1)}, f32[4,256,2304]{2,1,0:T(8,128)S(1)}) fusion(f32[256,2304]{1,0:T(8,128)S(1)} %get-tuple-element.139, f32[4]{0:T(128)S(1)} %fusion.50, bf16[8,2304,4,64]{1,3,2,0:T(8,128)(2,1)} %get-tuple-element.137, s32[]{:T(128)S(6)} %copy.42, bf16[8,256,4,64]{1,3,2,0:T(8,128)(2,1)} %get-tuple-element.136), kind=kOutput, calls=%fused_computation.44.clone.1 | convolution fusion | flops 311426048 | bytes 13112336 | tf_op jit(solution)/shard_map/while/body/eval_jaxpr/qgd,kgd->gqk/dot_general | solution.py:45
  219.6 2.9 %fusion.53 = bf16[8,256,4,64]{1,3,2,0:T(8,128)(2,1)S(1)} fusion(bf16[8,256,4,64]{1,3,2,0:T(8,128)(2,1)S(1)} %get-tuple-element.126, s32[]{:T(128)S(6)} %copy.42, f32[4,256,2304]{2,1,0:T(8,128)S(1)} %get-tuple-element.115, f32[4,256]{1,0:T(4,128)S(1)} %get-tuple-element.116, bf16[8,2304,4,64]{1,3,2,0:T(8,128)(2,1)} %get-tuple-element.135, ...), kind=kOutput, calls=%fused_computation.14.clone.1 | convolution fusion | flops 306839552 | bytes 10757120 | tf_op jit(solution)/shard_map/while/body/eval_jaxpr/gqk,kgd->qgd/dot_general | solution.py:51
  (75 shorter events, 26.3 us)
Async XLA Ops:
  0.0 87.1 %copy-start.11 = (s32[5]{0:T(128)S(1)}, s32[5]{0:T(128)}, u32[]{:S(2)}) copy-start(s32[5]{0:T(128)} %param.12) | copy-start | bytes 64
  0.0 94.2 %copy-start.9 = (bf16[256,2048]{1,0:T(8,128)(2,1)S(1)}, bf16[256,2048]{1,0:T(8,128)(2,1)}, u32[]{:S(2)}) copy-start(bf16[256,2048]{1,0:T(8,128)(2,1)} %param.8) | copy-start | bytes 3145732
  0.0 95.5 %copy-start.12 = (f32[32]{0:T(128)S(1)}, f32[32]{0:T(128)}, u32[]{:S(2)}) copy-start(f32[32]{0:T(128)} %param.13) | copy-start | bytes 388
  0.0 98.1 %copy-start.2 = (bf16[3,256,256]{2,1,0:T(8,128)(2,1)S(1)}, bf16[3,256,256]{2,1,0:T(8,128)(2,1)}, u32[]{:S(2)}) copy-start(bf16[3,256,256]{2,1,0:T(8,128)(2,1)} %param.11) | copy-start | bytes 1179652
  1.9 30.0 %collective-permute-start = (bf16[2,256,2048]{2,1,0:T(8,128)(2,1)S(1)}, bf16[2,256,2048]{2,1,0:T(8,128)(2,1)S(1)}, u32[]{:S(2)}, u32[]{:S(2)}) collective-permute-start(bf16[2,256,2048]{2,1,0:T(8,128)(2,1)S(1)} %pad_maximum_fusion), channel_id=1, source_target_pairs={{0,8},{8,16},{16,24},{24,32},{32,40},{40,48},{48,56},{56,64},{64,7... | collective-permute-start | bytes 6291464 | tf_op jit(solution)/shard_map/ppermute | solution.py:12
  2.0 29.9 %collective-permute-start.4 = (bf16[2,256,2048]{2,1,0:T(8,128)(2,1)S(1)}, bf16[2,256,2048]{2,1,0:T(8,128)(2,1)S(1)}, u32[]{:S(2)}, u32[]{:S(2)}) collective-permute-start(bf16[2,256,2048]{2,1,0:T(8,128)(2,1)S(1)} %pad_maximum_fusion), channel_id=1, source_target_pairs={{0,248},{8,0},{16,8},{24,16},{32,24},{40,32},{48,40},{56,48},{64,5... | collective-permute-start | bytes 6291464 | tf_op jit(solution)/shard_map/ppermute | solution.py:12
  31.9 28.8 %copy-start.5 = (bf16[2,256,2048]{2,1,0:T(8,128)(2,1)}, bf16[2,256,2048]{2,1,0:T(8,128)(2,1)S(1)}, u32[]{:S(2)}) copy-start(bf16[2,256,2048]{2,1,0:T(8,128)(2,1)S(1)} %collective-permute-done) | copy-start | bytes 6291460
  31.9 27.6 %collective-permute-start.1 = (bf16[2,256,2048]{2,1,0:T(8,128)(2,1)S(1)}, bf16[2,256,2048]{2,1,0:T(8,128)(2,1)S(1)}, u32[]{:S(2)}, u32[]{:S(2)}) collective-permute-start(bf16[2,256,2048]{2,1,0:T(8,128)(2,1)S(1)} %collective-permute-done), channel_id=1, source_target_pairs={{0,8},{8,16},{16,24},{24,32},{32,40},{40,48},{48,56},{56,64},{64,7... | collective-permute-start | bytes 6291464 | tf_op jit(solution)/shard_map/ppermute | solution.py:12
  31.9 1.3 copy-start.3
  33.2 27.5 %collective-permute-start.5 = (bf16[2,256,2048]{2,1,0:T(8,128)(2,1)S(1)}, bf16[2,256,2048]{2,1,0:T(8,128)(2,1)}, u32[]{:S(2)}, u32[]{:S(2)}) collective-permute-start(bf16[2,256,2048]{2,1,0:T(8,128)(2,1)S(1)} %collective-permute-done.4), channel_id=1, source_target_pairs={{0,248},{8,0},{16,8},{24,16},{32,24},{40,32},{48,40},{56,48},{64,5... | collective-permute-start | bytes 6291464 | tf_op jit(solution)/shard_map/ppermute | solution.py:12
  59.5 5.4 %copy-start.7 = (bf16[2,256,2048]{2,1,0:T(8,128)(2,1)}, bf16[2,256,2048]{2,1,0:T(8,128)(2,1)S(1)}, u32[]{:S(2)}) copy-start(bf16[2,256,2048]{2,1,0:T(8,128)(2,1)S(1)} %collective-permute-done.1) | copy-start | bytes 6291460
  59.5 27.7 %collective-permute-start.2 = (bf16[2,256,2048]{2,1,0:T(8,128)(2,1)S(1)}, bf16[2,256,2048]{2,1,0:T(8,128)(2,1)}, u32[]{:S(2)}, u32[]{:S(2)}) collective-permute-start(bf16[2,256,2048]{2,1,0:T(8,128)(2,1)S(1)} %collective-permute-done.1), channel_id=1, source_target_pairs={{0,8},{8,16},{16,24},{24,32},{32,40},{40,48},{48,56},{56,64},{64,7... | collective-permute-start | bytes 6291464 | tf_op jit(solution)/shard_map/ppermute | solution.py:12
  60.7 40.7 %collective-permute-start.6 = (bf16[2,256,2048]{2,1,0:T(8,128)(2,1)}, bf16[2,256,2048]{2,1,0:T(8,128)(2,1)}, u32[]{:S(2)}, u32[]{:S(2)}) collective-permute-start(bf16[2,256,2048]{2,1,0:T(8,128)(2,1)} %collective-permute-done.5), channel_id=1, source_target_pairs={{0,248},{8,0},{16,8},{24,16},{32,24},{40,32},{48,40},{56,48},{64,5... | collective-permute-start | bytes 6291464 | tf_op jit(solution)/shard_map/ppermute | solution.py:12
  87.1 27.9 %collective-permute-start.3 = (bf16[2,256,2048]{2,1,0:T(8,128)(2,1)}, bf16[2,256,2048]{2,1,0:T(8,128)(2,1)}, u32[]{:S(2)}, u32[]{:S(2)}) collective-permute-start(bf16[2,256,2048]{2,1,0:T(8,128)(2,1)} %collective-permute-done.2), channel_id=1, source_target_pairs={{0,8},{8,16},{16,24},{24,32},{32,40},{40,48},{48,56},{56,64},{64,7... | collective-permute-start | bytes 6291464 | tf_op jit(solution)/shard_map/ppermute | solution.py:12
  101.4 17.5 %copy-start.8 = (bf16[2,256,2048]{2,1,0:T(8,128)(2,1)S(1)}, bf16[2,256,2048]{2,1,0:T(8,128)(2,1)}, u32[]{:S(2)}) copy-start(bf16[2,256,2048]{2,1,0:T(8,128)(2,1)} %copy-done.7) | copy-start | bytes 6291460
  101.4 28.0 %collective-permute-start.7 = (bf16[2,256,2048]{2,1,0:T(8,128)(2,1)}, bf16[2,256,2048]{2,1,0:T(8,128)(2,1)S(1)}, u32[]{:S(2)}, u32[]{:S(2)}) collective-permute-start(bf16[2,256,2048]{2,1,0:T(8,128)(2,1)} %collective-permute-done.6), channel_id=1, source_target_pairs={{0,248},{8,0},{16,8},{24,16},{32,24},{40,32},{48,40},{56,48},{64,5... | collective-permute-start | bytes 6291464 | tf_op jit(solution)/shard_map/ppermute | solution.py:12
  116.9 2.2 copy-start.6
  118.9 1.3 copy-start
  118.9 1.6 copy-start.1
  119.1 2.1 copy-start.4
  149.7 12.8 %copy-start.10 = (bf16[8,256,4,64]{1,3,2,0:T(8,128)(2,1)S(1)}, bf16[8,256,4,64]{1,3,2,0:T(8,128)(2,1)}, u32[]{:S(2)}) copy-start(bf16[8,256,4,64]{1,3,2,0:T(8,128)(2,1)} %custom-call.2) | copy-start | bytes 3145732
where the time goes:
time: 225 us; the launch traced here: 224 us
  waiting for transfers between devices  83.4 us (37%)
  local copies, waits for them, and re-layouts  50 us (22%)
  matrix products  48.5 us (22%)
  starting transfers between devices  18.5 us (8%)
  other arithmetic  13.6 us (6%)
  between operations  9.84 us (4%)
    ppermute x8, waiting for transfers between devices, passed_along(): lax.ppermute(shard, axis, [(i, (i + by) % devices) for i in range(devices)])  83.4 us
    dot_general x8, matrix products, per_group(): jnp.einsum('qgd,kgd->gqk', query_one, key_one, preferred_element_type=jnp...  25.2 us
    dot_general x8, matrix products, per_group(): jnp.einsum('gqk,kgd->qgd', weights, value_one, preferred_element_type=jnp...  23.3 us
    slice x2, local copies, waits for them, and re-layouts, per_device(): window_pairs[0]  20 us
    ppermute x8, starting transfers between devices, passed_along(): lax.ppermute(shard, axis, [(i, (i + by) % devices) for i in range(devices)])  18.5 us
    unnamed x38, local copies, waits for them, and re-layouts  13.4 us
    slice x1, local copies, waits for them, and re-layouts, per_device(): window_pairs[1]  12.8 us
    reduce_sum x8, other arithmetic, per_group(): totals = jnp.sum(raised, axis=-1)  11.3 us
  transfers between devices with their start and end apart: 8, of which 6 were waited for; matrix products, arithmetic and copies ran while one was open for 6% of the time, Pallas kernels for 0%

commit v1 on v0

v1 whole, which is shorter than its diff:
```python
import functools
import math

import jax
import jax.numpy as jnp
from jax import lax
from jax.experimental import pallas as pl
from jax.experimental.pallas import tpu as pltpu
from jax.sharding import PartitionSpec as P

MESH = pl.DeviceIdType.MESH
HD = 64
WIN = 4
LANES = 128
LOG2E = math.log2(math.e)
AHEAD = 2

OWN, SIB, A_LOW, A_HIGH, B_LOW, B_HIGH, C_LOW, C_HIGH, FAR = range(9)
NEAR = (OWN, SIB, A_LOW, A_HIGH, B_LOW, B_HIGH)
OUTER = (C_LOW, C_HIGH, FAR)


def kernel(
    ring, buckets, slopes, q_hbm, k_hbm, v_hbm, tiles_hbm, out_ref,
    kv, q_buf, tiles, bias, send_sem, recv_sem, in_sem,
):
    groups, rows = kv.shape[0], kv.shape[3]
    me = lax.axis_index("seq")
    core = lax.rem(me, 2)
    up = lax.rem(me + 2, ring)
    down = lax.rem(me + ring - 2, ring)
    sib = me + 1 - 2 * core

    def columns(g):
        return pl.ds(pl.multiple_of(g * LANES, LANES), LANES)

    def remote(src, dst_slot, g, target):
        return pltpu.make_async_remote_copy(
            src_ref=src,
            dst_ref=kv.at[g, dst_slot],
            send_sem=send_sem.at[dst_slot, g],
            recv_sem=recv_sem.at[dst_slot, g],
            device_id={"seq": target},
            device_id_type=MESH,
        )

    def send_own(g, dst_slot, target):
        for part, ref in enumerate((k_hbm, v_hbm)):
            pltpu.make_async_remote_copy(
                src_ref=ref.at[:, columns(g)],
                dst_ref=kv.at[g, dst_slot, part],
                send_sem=send_sem.at[dst_slot, g],
                recv_sem=recv_sem.at[dst_slot, g],
                device_id={"seq": target},
                device_id_type=MESH,
            ).start()

    def send_own_all(g):
        send_own(g, A_LOW, up)
        send_own(g, A_HIGH, down)
        send_own(g, SIB, sib)

    def arrived(slot, g):
        remote(kv.at[g, slot], slot, g, sib).wait_recv()

    def forward(g):
        arrived(A_LOW, g)
        remote(kv.at[g, A_LOW], C_LOW, g, up).start()
        remote(kv.at[g, A_LOW], B_LOW, g, sib).start()
        arrived(A_HIGH, g)
        remote(kv.at[g, A_HIGH], C_HIGH, g, down).start()
        remote(kv.at[g, A_HIGH], B_HIGH, g, sib).start()

    barrier = pltpu.get_barrier_semaphore()
    for target in (up, down, sib):
        pl.semaphore_signal(barrier, inc=1, device_id={"seq": target}, device_id_type=MESH)
    pl.semaphore_wait(barrier, 3)

    for g in range(AHEAD):
        send_own_all(g)

    tiles_copy = pltpu.make_async_copy(tiles_hbm, tiles, in_sem.at[0])
    tiles_copy.start()

    @pl.loop(0, groups)
    def _(g):
        pltpu.make_async_copy(q_hbm.at[:, columns(g)], q_buf.at[g], in_sem.at[1]).start()
        pltpu.make_async_copy(k_hbm.at[:, columns(g)], kv.at[g, OWN, 0], in_sem.at[2]).start()
        pltpu.make_async_copy(v_hbm.at[:, columns(g)], kv.at[g, OWN, 1], in_sem.at[2]).start()

    tiles_copy.wait()
    for o in range(WIN + 1):
        tile = tiles[buckets[o]].astype(jnp.float32)
        bias[WIN + o] = tile
        if o > 0:
            bias[WIN - o] = tile.T
    pltpu.make_async_copy(q_buf, q_buf, in_sem.at[1]).wait()
    pltpu.make_async_copy(kv.at[:, OWN], kv.at[:, OWN], in_sem.at[2]).wait()

    offset = {
        OWN: 0,
        SIB: 1 - 2 * core,
        A_LOW: -2,
        A_HIGH: 2,
        B_LOW: -1 - 2 * core,
        B_HIGH: 3 - 2 * core,
        C_LOW: -4,
        C_HIGH: 4,
        FAR: 6 * core - 3,
    }
    lane_head = lax.broadcasted_iota(jnp.int32, (1, LANES), 1) // HD

    def scores(g, query, slope, slots):
        result = []
        for slot in slots:
            dots = lax.dot_general(
                query, kv[g, slot, 0], (((1,), (1,)), ((), ())),
                preferred_element_type=jnp.float32,
            )
            result.append(dots * LOG2E + slope * bias[offset[slot] + WIN])
        return result

    def row_max(parts):
        return jnp.max(functools.reduce(jnp.maximum, parts), axis=1, keepdims=True)

    def weighted(g, parts, peak, half, slots):
        total = None
        for part, slot in zip(parts, slots):
            weights = jnp.exp2(part - peak).astype(jnp.bfloat16)
            value = jnp.where(lane_head == half, kv[g, slot, 1], jnp.ones((), jnp.bfloat16))
            term = jnp.dot(weights, value, preferred_element_type=jnp.float32)
            total = term if total is None else total + term
        return total

    forward(0)

    @pl.loop(0, groups)
    def _(g):
        @pl.when(g + AHEAD < groups)
        def _():
            send_own_all(g + AHEAD)

        @pl.when(g + 1 < groups)
        def _():
            forward(g + 1)

        for slot in (SIB, B_LOW, B_HIGH):
            arrived(slot, g)
        query = q_buf[g] * jnp.asarray(HD ** -0.5, jnp.bfloat16)
        queries, slope, peaks, sums = [], [], [], []
        for half in range(2):
            queries.append(jnp.where(lane_head == half, query, jnp.zeros((), jnp.bfloat16)))
            slope.append(slopes[2 * g + half] * LOG2E)
            parts = scores(g, queries[half], slope[half], NEAR)
            peaks.append(row_max(parts))
            sums.append(weighted(g, parts, peaks[half], half, NEAR))

        mine = C_HIGH - core
        arrived(mine, g)
        remote(kv.at[g, mine], FAR, g, sib).start()
        arrived(C_LOW + core, g)
        arrived(FAR, g)
        totals = []
        for half in range(2):
            parts = scores(g, queries[half], slope[half], OUTER)
            peak = jnp.maximum(peaks[half], row_max(parts))
            totals.append(
                sums[half] * jnp.exp2(peaks[half] - peak)
                + weighted(g, parts, peak, half, OUTER)
            )
        first = lane_head == 0
        top = jnp.where(first, totals[0], totals[1])
        low = pltpu.roll(jnp.where(first, totals[1], totals[0]), HD, 1)
        out_ref[:, columns(g)] = (top / low).astype(out_ref.dtype)

    for slot, target in (
        (SIB, sib), (A_LOW, up), (A_HIGH, down), (B_LOW, sib), (B_HIGH, sib),
        (C_LOW, up), (C_HIGH, down), (FAR, sib),
    ):
        @pl.loop(0, groups)
        def _(g):
            remote(kv.at[g, slot], slot, g, target).wait_send()


def solution(mesh):
    ring = mesh.shape["seq"]

    def per_device(queries, key_rows, values, bias_tiles, buckets, slopes):
        rows, width = queries.shape
        groups = width // LANES
        return pl.pallas_call(
            functools.partial(kernel, ring),
            out_shape=jax.ShapeDtypeStruct((rows, width), queries.dtype),
            in_specs=[pl.BlockSpec(memory_space=pltpu.SMEM)] * 2
            + [pl.BlockSpec(memory_space=pl.ANY)] * 4,
            out_specs=pl.BlockSpec(memory_space=pltpu.VMEM),
            scratch_shapes=[
                pltpu.VMEM((groups, 9, 2, rows, LANES), jnp.bfloat16),
                pltpu.VMEM((groups, rows, LANES), jnp.bfloat16),
                pltpu.VMEM(bias_tiles.shape, jnp.bfloat16),
                pltpu.VMEM((2 * WIN + 1, rows, rows), jnp.float32),
                pltpu.SemaphoreType.DMA((9, groups)),
                pltpu.SemaphoreType.DMA((9, groups)),
                pltpu.SemaphoreType.DMA((3,)),
            ],
            compiler_params=pltpu.CompilerParams(
                collective_id=0, has_side_effects=True, vmem_limit_bytes=56 << 20
            ),
        )(buckets, slopes, queries, key_rows, values, bias_tiles)

    return jax.shard_map(
        per_device,
        mesh=mesh,
        in_specs=(P(("batch", "seq"), None),) * 3 + (P(), P(), P()),
        out_specs=P(("batch", "seq"), None),
        check_vma=False,
    )
```

time: 225 us -> 112 us (0.50)
  the two profiles are of different devices: /device:TPU:8 before, /device:TPU:1 now
where the time goes in v1:
time: 112 us
  Pallas kernels  110 us (98%)
  local copies, waits for them, and re-layouts  2.3 us (2%)
    pallas_call x1, Pallas kernels, per_device(): pl.pallas_call(functools.partial(kernel, ring), out_shape=jax.ShapeDtypeS...  110 us
    unnamed x1, local copies, waits for them, and re-layouts  2.3 us

profile of v1, /device:TPU:1, one launch (start us, length us, event | category | flops | bytes accessed | tf_op | source)
XLA Modules:
  0.0 112.1 jit_solution(7674574267925292950)
XLA Ops:
  0.0 109.7 %shard_map.64 = bf16[256,2048]{1,0:T(8,128)(2,1)} custom-call(s32[5]{0:T(128)} %buckets.1, f32[32]{0:T(128)} %slopes.1, bf16[256,2048]{1,0:T(8,128)(2,1)} %q_hbm.1, bf16[256,2048]{1,0:T(8,128)(2,1)} %k_hbm.1, bf16[256,2048]{1,0:T(8,128)(2,1)} %v_hbm.1, bf16[3,256,256]{2,1,0:T(8,128)(2,1)} %tiles_hbm.1), custom_call_target="tpu_custom_call" | custom-call | tf_op jit(solution)/shard_map/pallas_call | solution.py:191
  109.8 2.3 %copy.8 = bf16[256,2048]{1,0:T(8,128)(2,1)} copy(bf16[256,2048]{1,0:T(8,128)(2,1)} %shard_map.64) | data formatting | bytes 2097152

commit v2 on v1

v2 whole, which is shorter than its diff:
```python
import functools
import math

import jax
import jax.numpy as jnp
from jax import lax
from jax.experimental import pallas as pl
from jax.experimental.pallas import tpu as pltpu
from jax.sharding import PartitionSpec as P

MESH = pl.DeviceIdType.MESH
HD = 64
WIN = 4
LANES = 128
PACK = 16
LOG2E = math.log2(math.e)

OWN, SIB, A_LOW, A_HIGH, B_LOW, B_HIGH, C_LOW, C_HIGH, FAR = range(9)
NEAR = (OWN, SIB, A_LOW, A_HIGH, B_LOW, B_HIGH)
OUTER = (C_LOW, C_HIGH, FAR)


def kernel(
    ring, buckets, slopes, q_hbm, k_hbm, v_hbm, tiles_hbm, out_ref,
    kv, q_buf, k_buf, v_buf, tiles, bias, state, send_sem, recv_sem, in_sem,
):
    groups, rows = kv.shape[1], q_buf.shape[0]
    pieces = rows // PACK
    me = lax.axis_index("seq")
    core = lax.rem(me, 2)
    up = lax.rem(me + 2, ring)
    down = lax.rem(me + ring - 2, ring)
    sib = me + 1 - 2 * core

    def columns(g):
        return pl.ds(pl.multiple_of(g * LANES, LANES), LANES)

    def copy(src, dst, g, target):
        return pltpu.make_async_remote_copy(
            src_ref=kv.at[src, g],
            dst_ref=kv.at[dst, g],
            send_sem=send_sem.at[dst, g],
            recv_sem=recv_sem.at[dst, g],
            device_id={"seq": target},
            device_id_type=MESH,
        )

    def arrived(slot, g):
        copy(slot, slot, g, sib).wait_recv()

    loads = [
        pltpu.make_async_copy(src, dst, in_sem.at[i])
        for i, (src, dst) in enumerate(
            ((k_hbm, k_buf), (v_hbm, v_buf), (tiles_hbm, tiles), (q_hbm, q_buf))
        )
    ]
    for load in loads:
        load.start()

    barrier = pltpu.get_barrier_semaphore()
    for target in (up, down, sib):
        pl.semaphore_signal(barrier, inc=1, device_id={"seq": target}, device_id_type=MESH)
    pl.semaphore_wait(barrier, 3)
    loads[0].wait()
    loads[1].wait()

    @pl.loop(0, groups)
    def _(g):
        for half, buf in enumerate((k_buf, v_buf)):
            block = buf[:, columns(g)]
            for j in range(pieces):
                at = (half * pieces + j) * LANES
                kv[OWN, g, :, at : at + LANES] = block[j * PACK : (j + 1) * PACK]
        copy(OWN, A_LOW, g, up).start()
        copy(OWN, A_HIGH, g, down).start()
        copy(OWN, SIB, g, sib).start()

    def forward(g):
        arrived(A_LOW, g)
        copy(A_LOW, C_LOW, g, up).start()
        copy(A_LOW, B_LOW, g, sib).start()
        arrived(A_HIGH, g)
        copy(A_HIGH, C_HIGH, g, down).start()
        copy(A_HIGH, B_HIGH, g, sib).start()

    def share(g):
        mine = C_HIGH - core
        arrived(mine, g)
        copy(mine, FAR, g, sib).start()

    loads[2].wait()
    for o in range(WIN + 1):
        tile = tiles[buckets[o]].astype(jnp.float32)
        bias[WIN + o] = tile
        if o > 0:
            bias[WIN - o] = tile.T
    loads[3].wait()

    offset = {
        OWN: 0,
        SIB: 1 - 2 * core,
        A_LOW: -2,
        A_HIGH: 2,
        B_LOW: -1 - 2 * core,
        B_HIGH: 3 - 2 * core,
        C_LOW: -4,
        C_HIGH: 4,
        FAR: 6 * core - 3,
    }
    lane_head = lax.broadcasted_iota(jnp.int32, (1, LANES), 1) // HD
    first = lane_head == 0

    def block(slot, g, half):
        span = pieces * LANES
        packed = kv[slot, g, :, half * span : (half + 1) * span]
        return jnp.concatenate(
            [packed[:, j * LANES : (j + 1) * LANES] for j in range(pieces)], axis=0
        )

    def attend(g, slots):
        query = q_buf[:, columns(g)] * jnp.asarray(HD ** -0.5, jnp.bfloat16)
        totals, peaks = [], []
        for half in range(2):
            mask = lane_head == half
            chosen = jnp.where(mask, query, jnp.zeros((), jnp.bfloat16))
            slope = slopes[2 * g + half] * LOG2E
            scores = []
            for slot in slots:
                dots = lax.dot_general(
                    chosen, block(slot, g, 0), (((1,), (1,)), ((), ())),
                    preferred_element_type=jnp.float32,
                )
                scores.append(dots * LOG2E + slope * bias[offset[slot] + WIN])
            peak = jnp.max(functools.reduce(jnp.maximum, scores), axis=1, keepdims=True)
            total = None
            for score, slot in zip(scores, slots):
                weights = jnp.exp2(score - peak).astype(jnp.bfloat16)
                value = jnp.where(mask, block(slot, g, 1), jnp.ones((), jnp.bfloat16))
                term = jnp.dot(weights, value, preferred_element_type=jnp.float32)
                total = term if total is None else total + term
            totals.append(total)
            peaks.append(peak)
        top = jnp.where(first, totals[0], totals[1])
        low = pltpu.roll(jnp.where(first, totals[1], totals[0]), HD, 1)
        return top, low, jnp.where(first, peaks[0], peaks[1])

    forward(0)

    @pl.loop(0, groups)
    def _(g):
        @pl.when(g + 1 < groups)
        def _():
            forward(g + 1)

        for slot in (SIB, B_LOW, B_HIGH):
            arrived(slot, g)
        for i, value in enumerate(attend(g, NEAR)):
            state[g, i] = value

    share(0)

    @pl.loop(0, groups)
    def _(g):
        @pl.when(g + 1 < groups)
        def _():
            share(g + 1)

        arrived(C_LOW + core, g)
        arrived(FAR, g)
        top, low, peak = attend(g, OUTER)
        best = jnp.maximum(peak, state[g, 2])
        new, old = jnp.exp2(peak - best), jnp.exp2(state[g, 2] - best)
        result = (top * new + state[g, 0] * old) / (low * new + state[g, 1] * old)
        out_ref[:, columns(g)] = result.astype(out_ref.dtype)

    for slot, target in (
        (SIB, sib), (A_LOW, up), (A_HIGH, down), (B_LOW, sib), (B_HIGH, sib),
        (C_LOW, up), (C_HIGH, down), (FAR, sib),
    ):
        @pl.loop(0, groups)
        def _(g):
            copy(slot, slot, g, target).wait_send()


def solution(mesh):
    ring = mesh.shape["seq"]

    def per_device(queries, key_rows, values, bias_tiles, buckets, slopes):
        rows, width = queries.shape
        groups = width // LANES
        return pl.pallas_call(
            functools.partial(kernel, ring),
            out_shape=pltpu.VMEM((rows, width), queries.dtype),
            in_specs=[pl.BlockSpec(memory_space=pltpu.SMEM)] * 2
            + [pl.BlockSpec(memory_space=pl.ANY)] * 4,
            out_specs=pl.BlockSpec(memory_space=pltpu.VMEM),
            scratch_shapes=[
                pltpu.VMEM((9, groups, PACK, 2 * LANES * rows // PACK), jnp.bfloat16),
                pltpu.VMEM((rows, width), jnp.bfloat16),
                pltpu.VMEM((rows, width), jnp.bfloat16),
                pltpu.VMEM((rows, width), jnp.bfloat16),
                pltpu.VMEM(bias_tiles.shape, jnp.bfloat16),
                pltpu.VMEM((2 * WIN + 1, rows, rows), jnp.float32),
                pltpu.VMEM((groups, 3, rows, LANES), jnp.float32),
                pltpu.SemaphoreType.DMA((9, groups)),
                pltpu.SemaphoreType.DMA((9, groups)),
                pltpu.SemaphoreType.DMA((4,)),
            ],
            compiler_params=pltpu.CompilerParams(
                collective_id=0, has_side_effects=True, vmem_limit_bytes=56 << 20
            ),
        )(buckets, slopes, queries, key_rows, values, bias_tiles)

    return jax.shard_map(
        per_device,
        mesh=mesh,
        in_specs=(P(("batch", "seq"), None),) * 3 + (P(), P(), P()),
        out_specs=P(("batch", "seq"), None),
        check_vma=False,
    )
```

time: 112 us -> 107 us (0.955)
  Pallas kernels: 110 us -> 106 us
  local copies, waits for them, and re-layouts: 2.3 us -> 0.97 us
    pallas_call x1, Pallas kernels: 110 us -> 106 us  [per_device(): pl.pallas_call(functools.partial(kernel, ring), out_shape=pltpu.VMEM((row...]
    unnamed x1, local copies, waits for them, and re-layouts: 2.3 us -> 0.97 us
where the time goes in v2:
time: 107 us
  Pallas kernels  106 us (99%)
    pallas_call x1, Pallas kernels, per_device(): pl.pallas_call(functools.partial(kernel, ring), out_shape=pltpu.VMEM((row...  106 us

profile of v2, /device:TPU:1, one launch (start us, length us, event | category | flops | bytes accessed | tf_op | source)
XLA Modules:
  0.0 106.6 jit_solution(18289780138345384661)
XLA Ops:
  0.0 105.6 %shard_map.64 = bf16[256,2048]{1,0:T(8,128)(2,1)S(1)} custom-call(s32[5]{0:T(128)} %buckets.1, f32[32]{0:T(128)} %slopes.1, bf16[256,2048]{1,0:T(8,128)(2,1)} %q_hbm.1, bf16[256,2048]{1,0:T(8,128)(2,1)} %k_hbm.1, bf16[256,2048]{1,0:T(8,128)(2,1)} %v_hbm.1, bf16[3,256,256]{2,1,0:T(8,128)(2,1)} %tiles_hbm.1), custom_call_target="tpu_custom_call" | custom-call | tf_op jit(solution)/shard_map/pallas_call | solution.py:191
  105.7 1.0 copy.8

commit v3 on v2

v3 whole, which is shorter than its diff:
```python
import functools
import math

import jax
import jax.numpy as jnp
from jax import lax
from jax.experimental import pallas as pl
from jax.experimental.pallas import tpu as pltpu
from jax.sharding import PartitionSpec as P

MESH = pl.DeviceIdType.MESH
HD = 64
WIN = 4
LANES = 128
LOG2E = math.log2(math.e)

OWN, SIB, A_LOW, A_HIGH, B_LOW, B_HIGH, C_LOW, C_HIGH, FAR = range(9)


def kernel(
    ring, buckets_hbm, slopes_hbm, q_hbm, k_hbm, v_hbm, tiles_hbm, out_ref,
    kv, q_buf, tiles, bias, state, buckets, slopes, send_sem, recv_sem, in_sem,
):
    groups = q_buf.shape[1] // LANES
    me = lax.axis_index("seq")
    core = lax.rem(me, 2)
    up = lax.rem(me + 2, ring)
    down = lax.rem(me + ring - 2, ring)
    sib = me + 1 - 2 * core
    own_chunks = spans(groups, (4, 4, 4))
    far_chunks = spans(groups, (4, 4, 2, 2, 1, 1, 1))
    target = (lax.rem(me + ring - 2 + 4 * core, ring), lax.rem(me + 2 + ring - 4 * core, ring))
    near_slot = (A_HIGH - core, A_LOW + core)
    sib_slot = (B_HIGH - core, B_LOW + core)
    far_slot = (C_HIGH - core, C_LOW + core)

    def columns(g, count=1):
        return pl.ds(pl.multiple_of(g * LANES, LANES), count * LANES)

    def remote(src, slot, chunk, part, i, device):
        return pltpu.make_async_remote_copy(
            src_ref=src.at[:, columns(*chunk)],
            dst_ref=kv.at[slot, part, :, columns(*chunk)],
            send_sem=send_sem.at[slot, part, i],
            recv_sem=recv_sem.at[slot, part, i],
            device_id={"seq": device},
            device_id_type=MESH,
        )

    def send_own(i, slot, device):
        for part, ref in enumerate((k_hbm, v_hbm)):
            remote(ref, slot, own_chunks[i], part, i, device).start()

    def pass_on(src, slot, chunks, i, device):
        for part in range(2):
            remote(kv.at[src, part], slot, chunks[i], part, i, device).start()

    def arrived(slot, chunks, i):
        for part in range(2):
            remote(kv.at[slot, part], slot, chunks[i], part, i, sib).wait_recv()

    def signal(semaphore, device):
        pl.semaphore_signal(semaphore, inc=1, device_id={"seq": device}, device_id_type=MESH)

    loads = [
        pltpu.make_async_copy(src, dst, in_sem.at[i])
        for i, (src, dst) in enumerate((
            (buckets_hbm, buckets), (tiles_hbm, tiles), (slopes_hbm, slopes), (q_hbm, q_buf),
            (k_hbm, kv.at[OWN, 0]), (v_hbm, kv.at[OWN, 1]),
        ))
    ]
    barrier = pltpu.get_barrier_semaphore()
    for device in (up, down, sib):
        signal(barrier, device)
    for load in loads:
        load.start()
    pl.semaphore_wait(barrier, 3)

    def start_stream(stream):
        for i in range(len(own_chunks)):
            send_own(i, near_slot[stream], target[stream])

    start_stream(0)
    for i in range(len(own_chunks)):
        send_own(i, SIB, sib)

    loads[0].wait()
    loads[1].wait()
    for o in range(WIN + 1):
        tile = tiles[buckets[o]].astype(jnp.float32)
        bias[WIN + o] = tile
        if o > 0:
            bias[WIN - o] = tile.T

    remote(k_hbm, near_slot[0], own_chunks[0], 0, 0, sib).wait_send()
    start_stream(1)
    for load in loads[2:]:
        load.wait()

    lane_head = lax.broadcasted_iota(jnp.int32, (1, LANES), 1) // HD
    first = lane_head == 0
    near = (
        (OWN, 0), (SIB, 1 - 2 * core), (A_LOW, -2), (A_HIGH, 2),
        (B_LOW, -1 - 2 * core), (B_HIGH, 3 - 2 * core),
    )
    outer = ((C_LOW, -4), (C_HIGH, 4), (FAR, 6 * core - 3))

    def attend(g, blocks):
        query = q_buf[:, columns(g)] * jnp.asarray(HD ** -0.5, jnp.bfloat16)
        totals, peaks = [], []
        for half in range(2):
            mask = lane_head == half
            chosen = jnp.where(mask, query, jnp.zeros((), jnp.bfloat16))
            slope = slopes[2 * g + half] * LOG2E
            scores = []
            for slot, offset in blocks:
                dots = lax.dot_general(
                    chosen, kv[slot, 0, :, columns(g)], (((1,), (1,)), ((), ())),
                    preferred_element_type=jnp.float32,
                )
                scores.append(dots * LOG2E + slope * bias[offset + WIN])
            peak = jnp.max(functools.reduce(jnp.maximum, scores), axis=1, keepdims=True)
            total = None
            for score, (slot, _) in zip(scores, blocks):
                weights = jnp.exp2(score - peak).astype(jnp.bfloat16)
                value = jnp.where(mask, kv[slot, 1, :, columns(g)], jnp.ones((), jnp.bfloat16))
                term = jnp.dot(weights, value, preferred_element_type=jnp.float32)
                total = term if total is None else total + term
            totals.append(total)
            peaks.append(peak)
        top = jnp.where(first, totals[0], totals[1])
        low = pltpu.roll(jnp.where(first, totals[1], totals[0]), HD, 1)
        return top, low, jnp.where(first, peaks[0], peaks[1])

    def merged(g, part):
        top, low, peak = part
        best = jnp.maximum(peak, state[g, 2])
        new, old = jnp.exp2(peak - best), jnp.exp2(state[g, 2] - best)
        return top * new + state[g, 0] * old, low * new + state[g, 1] * old, best

    def keep(g, part):
        for i, value in enumerate(part):
            state[g, i] = value

    def at_start(g, chunks, act):
        for i, (start, _) in enumerate(chunks):
            @pl.when(g == start)
            def _():
                act(i)

    def relay(i):
        start, count = own_chunks[i]
        for stream in range(2):
            arrived(near_slot[stream], own_chunks, i)
            for j, (inner, _) in enumerate(far_chunks):
                if start <= inner < start + count:
                    pass_on(near_slot[stream], far_slot[stream], far_chunks, j, target[stream])
            pass_on(near_slot[stream], sib_slot[stream], own_chunks, i, sib)
        for slot in (SIB, B_LOW, B_HIGH):
            arrived(slot, own_chunks, i)

    @pl.loop(0, groups)
    def _(g):
        at_start(g, own_chunks, relay)
        keep(g, attend(g, near))

    def share(j):
        for part in range(2):
            mine = far_slot[0]
            remote(kv.at[mine, part], mine, far_chunks[j], part, j, sib).wait_recv()
            remote(kv.at[mine, part], FAR, far_chunks[j], part, j, sib).start()

    shares = ((0,), (1, 2), (3,), (4, 5), (6,), (7,), (), ())

    def prepare(j):
        for ahead in shares[j]:
            share(ahead)
        arrived(far_slot[1], far_chunks, j)
        arrived(FAR, far_chunks, j)

    @pl.loop(0, groups)
    def _(g):
        at_start(g, far_chunks, prepare)
        top, low, _ = merged(g, attend(g, outer))
        out_ref[:, columns(g)] = (top / low).astype(out_ref.dtype)

    for slot, chunks in (
        (SIB, own_chunks), (near_slot[0], own_chunks), (near_slot[1], own_chunks),
        (B_LOW, own_chunks), (B_HIGH, own_chunks), (C_LOW, far_chunks), (C_HIGH, far_chunks),
        (FAR, far_chunks),
    ):
        for i in range(len(chunks)):
            for part in range(2):
                if slot is near_slot[0] and i == part == 0:
                    continue
                remote(kv.at[slot, part], slot, chunks[i], part, i, sib).wait_send()


def spans(groups, sizes):
    starts = [sum(sizes[:i]) for i in range(len(sizes))]
    result = [(a, n) for a, n in zip(starts, sizes) if a + n < groups]
    done = sum(n for _, n in result)
    return result + [(done, groups - done)]


def solution(mesh):
    ring = mesh.shape["seq"]

    def per_device(queries, key_rows, values, bias_tiles, buckets, slopes):
        rows, width = queries.shape
        groups = width // LANES
        return pl.pallas_call(
            functools.partial(kernel, ring),
            out_shape=pltpu.VMEM((rows, width), queries.dtype),
            in_specs=[pl.BlockSpec(memory_space=pl.ANY)] * 6,
            out_specs=pl.BlockSpec(memory_space=pltpu.VMEM),
            scratch_shapes=[
                pltpu.VMEM((9, 2, rows, width), jnp.bfloat16),
                pltpu.VMEM((rows, width), jnp.bfloat16),
                pltpu.VMEM(bias_tiles.shape, jnp.bfloat16),
                pltpu.VMEM((2 * WIN + 1, rows, rows), jnp.float32),
                pltpu.VMEM((groups, 3, rows, LANES), jnp.float32),
                pltpu.SMEM(buckets.shape, jnp.int32),
                pltpu.SMEM(slopes.shape, jnp.float32),
                pltpu.SemaphoreType.DMA((9, 2, 8)),
                pltpu.SemaphoreType.DMA((9, 2, 8)),
                pltpu.SemaphoreType.DMA((6,)),
            ],
            compiler_params=pltpu.CompilerParams(
                collective_id=0, has_side_effects=True, vmem_limit_bytes=56 << 20
            ),
        )(buckets, slopes, queries, key_rows, values, bias_tiles)

    return jax.shard_map(
        per_device,
        mesh=mesh,
        in_specs=(P(("batch", "seq"), None),) * 3 + (P(), P(), P()),
        out_specs=P(("batch", "seq"), None),
        check_vma=False,
    )
```

time: 107 us -> 104 us (0.972)
  Pallas kernels: 106 us -> 103 us
    pallas_call x1, Pallas kernels: 106 us -> 103 us  [per_device(): pl.pallas_call(functools.partial(kernel, ring), out_shape=pltpu.VMEM((row...]
where the time goes in v3:
time: 104 us
  Pallas kernels  103 us (99%)
    pallas_call x1, Pallas kernels, per_device(): pl.pallas_call(functools.partial(kernel, ring), out_shape=pltpu.VMEM((row...  103 us

profile of v3, /device:TPU:1, one launch (start us, length us, event | category | flops | bytes accessed | tf_op | source)
XLA Modules:
  0.0 103.9 jit_solution(10154745860408708782)
XLA Ops:
  0.0 102.9 %shard_map.64 = bf16[256,2048]{1,0:T(8,128)(2,1)S(1)} custom-call(s32[5]{0:T(128)} %buckets_hbm.1, f32[32]{0:T(128)} %slopes_hbm.1, bf16[256,2048]{1,0:T(8,128)(2,1)} %q_hbm.1, bf16[256,2048]{1,0:T(8,128)(2,1)} %k_hbm.1, bf16[256,2048]{1,0:T(8,128)(2,1)} %v_hbm.1, bf16[3,256,256]{2,1,0:T(8,128)(2,1)} %tiles_hbm.1), custom_call_target="tpu_custom_call" | custom-call | tf_op jit(solution)/shard_map/pallas_call | solution.py:212
  102.9 1.0 copy.8

commit v4 on v3

v4 whole, which is shorter than its diff:
```python
import functools
import math

import jax
import jax.numpy as jnp
from jax import lax
from jax.experimental import pallas as pl
from jax.experimental.pallas import tpu as pltpu
from jax.sharding import PartitionSpec as P

MESH = pl.DeviceIdType.MESH
HD = 64
WIN = 4
LANES = 128
LOG2E = math.log2(math.e)

OWN, SIB, A_LOW, A_HIGH, B_LOW, B_HIGH, C_LOW, C_HIGH, FAR = range(9)


def kernel(
    ring, buckets_hbm, slopes_hbm, q_hbm, k_hbm, v_hbm, tiles_hbm, out_ref,
    kv, q_buf, tiles, bias, state, sums, buckets, slopes, send_sem, recv_sem, in_sem, lead_sem,
):
    groups = q_buf.shape[1] // LANES
    me = lax.axis_index("seq")
    core = lax.rem(me, 2)
    up = lax.rem(me + 2, ring)
    down = lax.rem(me + ring - 2, ring)
    sib = me + 1 - 2 * core
    own_chunks = spans(groups, (4, 4, 4))
    far_chunks = spans(groups, (4, 4, 2, 2, 1, 1, 1))
    target = (lax.rem(me + ring - 2 + 4 * core, ring), lax.rem(me + 2 + ring - 4 * core, ring))
    near_slot = (A_HIGH - core, A_LOW + core)
    sib_slot = (B_HIGH - core, B_LOW + core)
    far_slot = (C_HIGH - core, C_LOW + core)

    def columns(g, count=1):
        return pl.ds(pl.multiple_of(g * LANES, LANES), count * LANES)

    def remote(src, dst, send, recv, device):
        return pltpu.make_async_remote_copy(
            src_ref=src, dst_ref=dst, send_sem=send, recv_sem=recv,
            device_id={"seq": device}, device_id_type=MESH,
        )

    def send_own(i, slot, device, first_sem=None):
        for part, ref in enumerate((k_hbm, v_hbm)):
            span = columns(*own_chunks[i])
            send = send_sem.at[slot, i] if first_sem is None or part else first_sem
            remote(
                ref.at[:, span], kv.at[slot, part, :, span], send, recv_sem.at[slot, i], device
            ).start()

    def passing(src, slot, chunks, i, device):
        span = columns(*chunks[i])
        return remote(
            kv.at[src, :, :, span], kv.at[slot, :, :, span],
            send_sem.at[slot, i], recv_sem.at[slot, i], device,
        )

    def arrived(slot, chunks, i):
        passing(slot, slot, chunks, i, sib).wait_recv()

    def left(slot, chunks, i):
        passing(slot, slot, chunks, i, sib).wait_send()

    def signal(semaphore, device):
        pl.semaphore_signal(semaphore, inc=1, device_id={"seq": device}, device_id_type=MESH)

    loads = [
        pltpu.make_async_copy(src, dst, in_sem.at[i])
        for i, (src, dst) in enumerate((
            (buckets_hbm, buckets), (tiles_hbm, tiles), (slopes_hbm, slopes), (q_hbm, q_buf),
            (k_hbm, kv.at[OWN, 0]), (v_hbm, kv.at[OWN, 1]),
        ))
    ]
    barrier = pltpu.get_barrier_semaphore()
    for device in (up, down, sib):
        signal(barrier, device)
    for load in loads:
        load.start()
    pl.semaphore_wait(barrier, 3)

    def start_stream(stream):
        for i in range(len(own_chunks)):
            send_own(
                i, near_slot[stream], target[stream], lead_sem if i == stream == 0 else None
            )

    start_stream(0)
    for i in range(len(own_chunks)):
        send_own(i, SIB, sib)

    loads[0].wait()
    loads[1].wait()
    for o in range(WIN + 1):
        tile = tiles[buckets[o]].astype(jnp.float32)
        bias[WIN + o] = tile.T
        if o > 0:
            bias[WIN - o] = tile

    head = columns(*own_chunks[0])
    remote(
        k_hbm.at[:, head], kv.at[OWN, 0, :, head], lead_sem, recv_sem.at[OWN, 0], sib
    ).wait_send()
    start_stream(1)
    for load in loads[2:]:
        load.wait()

    lane_head = lax.broadcasted_iota(jnp.int32, (1, LANES), 1) // HD
    near = (
        (OWN, 0), (SIB, 1 - 2 * core), (A_LOW, -2), (A_HIGH, 2),
        (B_LOW, -1 - 2 * core), (B_HIGH, 3 - 2 * core),
    )
    outer = ((C_LOW, -4), (C_HIGH, 4), (FAR, 6 * core - 3))

    def attend(g, blocks):
        query = q_buf[:, columns(g)] * jnp.asarray(HD ** -0.5, jnp.bfloat16)
        totals, peaks = [], []
        for half in range(2):
            mask = lane_head == half
            chosen = jnp.where(mask, query, jnp.zeros((), jnp.bfloat16))
            slope = slopes[2 * g + half] * LOG2E
            scores = []
            for slot, offset in blocks:
                dots = lax.dot_general(
                    kv[slot, 0, :, columns(g)], chosen, (((1,), (1,)), ((), ())),
                    preferred_element_type=jnp.float32,
                )
                scores.append(dots * LOG2E + slope * bias[offset + WIN])
            peak = jnp.max(functools.reduce(jnp.maximum, scores), axis=0, keepdims=True)
            total = None
            for score, (slot, _) in zip(scores, blocks):
                weights = jnp.exp2(score - peak).astype(jnp.bfloat16)
                value = jnp.where(mask, kv[slot, 1, :, columns(g)], jnp.ones((), jnp.bfloat16))
                term = lax.dot_general(
                    value, weights, (((0,), (0,)), ((), ())), preferred_element_type=jnp.float32
                )
                total = term if total is None else total + term
            totals.append(total)
            peaks.append(peak)
        tops = totals[0][:HD], totals[1][HD:]
        lows = totals[0][HD : HD + 1], totals[1][:1]
        return tops, lows, peaks

    def keep(g, part):
        tops, lows, peaks = part
        for half in range(2):
            state[g, half * HD : (half + 1) * HD] = tops[half]
            sums[g, half : half + 1] = lows[half]
            sums[g, half + 2 : half + 3] = peaks[half]

    def finish(g, part):
        tops, lows, peaks = part
        results = []
        for half in range(2):
            old_peak = sums[g, half + 2 : half + 3]
            best = jnp.maximum(peaks[half], old_peak)
            new, old = jnp.exp2(peaks[half] - best), jnp.exp2(old_peak - best)
            low = lows[half] * new + sums[g, half : half + 1] * old
            top = tops[half] * new + state[g, half * HD : (half + 1) * HD] * old
            results.append(top / low)
        out_ref[:, columns(g)] = jnp.concatenate(results, axis=0).T.astype(out_ref.dtype)

    def at_start(g, chunks, act):
        for i, (start, _) in enumerate(chunks):
            @pl.when(g == start)
            def _():
                act(i)

    def relay(i):
        start, count = own_chunks[i]
        for stream in range(2):
            arrived(near_slot[stream], own_chunks, i)
            for j, (inner, _) in enumerate(far_chunks):
                if start <= inner < start + count:
                    passing(
                        near_slot[stream], far_slot[stream], far_chunks, j, target[stream]
                    ).start()
            passing(near_slot[stream], sib_slot[stream], own_chunks, i, sib).start()
        for slot in (SIB, B_LOW, B_HIGH):
            arrived(slot, own_chunks, i)

    @pl.loop(0, groups)
    def _(g):
        at_start(g, own_chunks, relay)
        keep(g, attend(g, near))

    def share(j):
        arrived(far_slot[0], far_chunks, j)
        passing(far_slot[0], FAR, far_chunks, j, sib).start()

    for i in range(len(own_chunks)):
        for slot in (SIB, near_slot[1], B_LOW, B_HIGH):
            left(slot, own_chunks, i)
        if i > 0:
            left(near_slot[0], own_chunks, i)
    remote(
        v_hbm.at[:, head], kv.at[OWN, 1, :, head],
        send_sem.at[near_slot[0], 0], recv_sem.at[OWN, 0], sib,
    ).wait_send()

    shares = ((0,), (1, 2), (3,), (4, 5), (6,), (7,), (), ())

    def prepare(j):
        for ahead in shares[j]:
            share(ahead)
        arrived(far_slot[1], far_chunks, j)
        arrived(FAR, far_chunks, j)
        if j > 0:
            for slot in (C_LOW, C_HIGH, FAR):
                left(slot, far_chunks, j - 1)

    @pl.loop(0, groups)
    def _(g):
        at_start(g, far_chunks, prepare)
        finish(g, attend(g, outer))

    for slot in (C_LOW, C_HIGH, FAR):
        left(slot, far_chunks, len(far_chunks) - 1)


def spans(groups, sizes):
    starts = [sum(sizes[:i]) for i in range(len(sizes))]
    result = [(a, n) for a, n in zip(starts, sizes) if a + n < groups]
    done = sum(n for _, n in result)
    return result + [(done, groups - done)]


def solution(mesh):
    ring = mesh.shape["seq"]

    def per_device(queries, key_rows, values, bias_tiles, buckets, slopes):
        rows, width = queries.shape
        groups = width // LANES
        return pl.pallas_call(
            functools.partial(kernel, ring),
            out_shape=pltpu.VMEM((rows, width), queries.dtype),
            in_specs=[pl.BlockSpec(memory_space=pl.ANY)] * 6,
            out_specs=pl.BlockSpec(memory_space=pltpu.VMEM),
            scratch_shapes=[
                pltpu.VMEM((9, 2, rows, width), jnp.bfloat16),
                pltpu.VMEM((rows, width), jnp.bfloat16),
                pltpu.VMEM(bias_tiles.shape, jnp.bfloat16),
                pltpu.VMEM((2 * WIN + 1, rows, rows), jnp.float32),
                pltpu.VMEM((groups, LANES, rows), jnp.float32),
                pltpu.VMEM((groups, 8, rows), jnp.float32),
                pltpu.SMEM(buckets.shape, jnp.int32),
                pltpu.SMEM(slopes.shape, jnp.float32),
                pltpu.SemaphoreType.DMA((9, 8)),
                pltpu.SemaphoreType.DMA((9, 8)),
                pltpu.SemaphoreType.DMA((6,)),
                pltpu.SemaphoreType.DMA,
            ],
            compiler_params=pltpu.CompilerParams(
                collective_id=0, has_side_effects=True, vmem_limit_bytes=56 << 20
            ),
        )(buckets, slopes, queries, key_rows, values, bias_tiles)

    return jax.shard_map(
        per_device,
        mesh=mesh,
        in_specs=(P(("batch", "seq"), None),) * 3 + (P(), P(), P()),
        out_specs=P(("batch", "seq"), None),
        check_vma=False,
    )
```

time: 104 us -> 102 us (0.981)
  Pallas kernels: 103 us -> 101 us
    pallas_call x1, Pallas kernels: 103 us -> 101 us  [per_device(): pl.pallas_call(functools.partial(kernel, ring), out_shape=pltpu.VMEM((row...]
where the time goes in v4:
time: 102 us
  Pallas kernels  101 us (99%)
    pallas_call x1, Pallas kernels, per_device(): pl.pallas_call(functools.partial(kernel, ring), out_shape=pltpu.VMEM((row...  101 us

profile of v4, /device:TPU:1, one launch (start us, length us, event | category | flops | bytes accessed | tf_op | source)
XLA Modules:
  0.0 102.2 jit_solution(1143016736408882597)
XLA Ops:
  0.0 101.2 %shard_map.64 = bf16[256,2048]{1,0:T(8,128)(2,1)S(1)} custom-call(s32[5]{0:T(128)} %buckets_hbm.1, f32[32]{0:T(128)} %slopes_hbm.1, bf16[256,2048]{1,0:T(8,128)(2,1)} %q_hbm.1, bf16[256,2048]{1,0:T(8,128)(2,1)} %k_hbm.1, bf16[256,2048]{1,0:T(8,128)(2,1)} %v_hbm.1, bf16[3,256,256]{2,1,0:T(8,128)(2,1)} %tiles_hbm.1), custom_call_target="tpu_custom_call" | custom-call | tf_op jit(solution)/shard_map/pallas_call | solution.py:236
  101.2 1.0 copy.8

commit v5 on v4

--- a/solution.py
+++ b/solution.py
@@ -19,7 +19,7 @@
 
 def kernel(
     ring, buckets_hbm, slopes_hbm, q_hbm, k_hbm, v_hbm, tiles_hbm, out_ref,
-    kv, q_buf, tiles, bias, state, sums, buckets, slopes, send_sem, recv_sem, in_sem, lead_sem,
+    kv, q_buf, tiles, bias, state, sums, buckets, slopes, send_sem, near_sem, far_sem, in_sem, lead_sem,
 ):
     groups = q_buf.shape[1] // LANES
     me = lax.axis_index("seq")
@@ -27,8 +27,8 @@
     up = lax.rem(me + 2, ring)
     down = lax.rem(me + ring - 2, ring)
     sib = me + 1 - 2 * core
-    own_chunks = spans(groups, (4, 4, 4))
-    far_chunks = spans(groups, (4, 4, 2, 2, 1, 1, 1))
+    own_chunks = spans(groups, (2, 2, 4, 4))
+    far_chunks = spans(groups, (2, 2, 4, 2, 2, 1, 1, 1))
     target = (lax.rem(me + ring - 2 + 4 * core, ring), lax.rem(me + 2 + ring - 4 * core, ring))
     near_slot = (A_HIGH - core, A_LOW + core)
     sib_slot = (B_HIGH - core, B_LOW + core)
@@ -43,26 +43,31 @@
             device_id={"seq": device}, device_id_type=MESH,
         )
 
+    def recv_sem(slot, chunks, i):
+        return near_sem.at[slot - SIB, i] if chunks is own_chunks else far_sem.at[slot - C_LOW, i]
+
     def send_own(i, slot, device, first_sem=None):
         for part, ref in enumerate((k_hbm, v_hbm)):
             span = columns(*own_chunks[i])
-            send = send_sem.at[slot, i] if first_sem is None or part else first_sem
+            send = send_sem.at[slot] if first_sem is None or part else first_sem
             remote(
-                ref.at[:, span], kv.at[slot, part, :, span], send, recv_sem.at[slot, i], device
+                ref.at[:, span], kv.at[slot, part, :, span],
+                send, recv_sem(slot, own_chunks, i), device,
             ).start()
 
     def passing(src, slot, chunks, i, device):
         span = columns(*chunks[i])
         return remote(
             kv.at[src, :, :, span], kv.at[slot, :, :, span],
-            send_sem.at[slot, i], recv_sem.at[slot, i], device,
+            send_sem.at[slot], recv_sem(slot, chunks, i), device,
         )
 
     def arrived(slot, chunks, i):
         passing(slot, slot, chunks, i, sib).wait_recv()
 
-    def left(slot, chunks, i):
-        passing(slot, slot, chunks, i, sib).wait_send()
+    def left(slot, count=None):
+        whole = kv.at[slot, :, :, : (count or groups) * LANES]
+        remote(whole, whole, send_sem.at[slot], near_sem.at[0, 0], sib).wait_send()
 
     def signal(semaphore, device):
         pl.semaphore_signal(semaphore, inc=1, device_id={"seq": device}, device_id_type=MESH)
@@ -101,7 +106,7 @@
 
     head = columns(*own_chunks[0])
     remote(
-        k_hbm.at[:, head], kv.at[OWN, 0, :, head], lead_sem, recv_sem.at[OWN, 0], sib
+        k_hbm.at[:, head], kv.at[OWN, 0, :, head], lead_sem, near_sem.at[0, 0], sib
     ).wait_send()
     start_stream(1)
     for load in loads[2:]:
@@ -190,26 +195,17 @@
         arrived(far_slot[0], far_chunks, j)
         passing(far_slot[0], FAR, far_chunks, j, sib).start()
 
-    for i in range(len(own_chunks)):
-        for slot in (SIB, near_slot[1], B_LOW, B_HIGH):
-            left(slot, own_chunks, i)
-        if i > 0:
-            left(near_slot[0], own_chunks, i)
-    remote(
-        v_hbm.at[:, head], kv.at[OWN, 1, :, head],
-        send_sem.at[near_slot[0], 0], recv_sem.at[OWN, 0], sib,
-    ).wait_send()
-
-    shares = ((0,), (1, 2), (3,), (4, 5), (6,), (7,), (), ())
+    for slot in (SIB, near_slot[1], B_LOW, B_HIGH):
+        left(slot)
+    left(near_slot[0], groups - own_chunks[0][1] // 2)
+
+    shares = ((0,), (1,), (2, 3), (4,), (5, 6), (7,), (8,), (), ())
 
     def prepare(j):
         for ahead in shares[j]:
             share(ahead)
         arrived(far_slot[1], far_chunks, j)
         arrived(FAR, far_chunks, j)
-        if j > 0:
-            for slot in (C_LOW, C_HIGH, FAR):
-                left(slot, far_chunks, j - 1)
 
     @pl.loop(0, groups)
     def _(g):
@@ -217,7 +213,7 @@
         finish(g, attend(g, outer))
 
     for slot in (C_LOW, C_HIGH, FAR):
-        left(slot, far_chunks, len(far_chunks) - 1)
+        left(slot)
 
 
 def spans(groups, sizes):
@@ -247,8 +243,9 @@
                 pltpu.VMEM((groups, 8, rows), jnp.float32),
                 pltpu.SMEM(buckets.shape, jnp.int32),
                 pltpu.SMEM(slopes.shape, jnp.float32),
-                pltpu.SemaphoreType.DMA((9, 8)),
-                pltpu.SemaphoreType.DMA((9, 8)),
+                pltpu.SemaphoreType.DMA((9,)),
+                pltpu.SemaphoreType.DMA((5, 5)),
+                pltpu.SemaphoreType.DMA((3, 9)),
                 pltpu.SemaphoreType.DMA((6,)),
                 pltpu.SemaphoreType.DMA,
             ],

time: 102 us -> 101 us (level)
  Pallas kernels: 101 us -> 99.7 us
    pallas_call x1, Pallas kernels: 101 us -> 99.7 us  [per_device(): pl.pallas_call(functools.partial(kernel, ring), out_shape=pltpu.VMEM((row...]
where the time goes in v5:
time: 101 us
  Pallas kernels  99.7 us (99%)
    pallas_call x1, Pallas kernels, per_device(): pl.pallas_call(functools.partial(kernel, ring), out_shape=pltpu.VMEM((row...  99.7 us

profile of v5, /device:TPU:1, one launch (start us, length us, event | category | flops | bytes accessed | tf_op | source)
XLA Modules:
  0.0 100.7 jit_solution(17094256762161958603)
XLA Ops:
  0.0 99.7 %shard_map.64 = bf16[256,2048]{1,0:T(8,128)(2,1)S(1)} custom-call(s32[5]{0:T(128)} %buckets_hbm.1, f32[32]{0:T(128)} %slopes_hbm.1, bf16[256,2048]{1,0:T(8,128)(2,1)} %q_hbm.1, bf16[256,2048]{1,0:T(8,128)(2,1)} %k_hbm.1, bf16[256,2048]{1,0:T(8,128)(2,1)} %v_hbm.1, bf16[3,256,256]{2,1,0:T(8,128)(2,1)} %tiles_hbm.1), custom_call_target="tpu_custom_call" | custom-call | tf_op jit(solution)/shard_map/pallas_call | solution.py:232
  99.7 1.0 copy.8

commit v6 on v5

--- a/solution.py
+++ b/solution.py
@@ -29,6 +29,7 @@
     sib = me + 1 - 2 * core
     own_chunks = spans(groups, (2, 2, 4, 4))
     far_chunks = spans(groups, (2, 2, 4, 2, 2, 1, 1, 1))
+    last = len(far_chunks) - 1
     target = (lax.rem(me + ring - 2 + 4 * core, ring), lax.rem(me + 2 + ring - 4 * core, ring))
     near_slot = (A_HIGH - core, A_LOW + core)
     sib_slot = (B_HIGH - core, B_LOW + core)
@@ -60,6 +61,13 @@
         return remote(
             kv.at[src, :, :, span], kv.at[slot, :, :, span],
             send_sem.at[slot], recv_sem(slot, chunks, i), device,
+        )
+
+    def final(src, slot, part, device):
+        span = columns(*far_chunks[last])
+        return remote(
+            kv.at[src, part, :, span], kv.at[slot, part, :, span],
+            send_sem.at[slot], far_sem.at[slot - C_LOW, last + part], device,
         )
 
     def arrived(slot, chunks, i):
@@ -119,12 +127,11 @@
     )
     outer = ((C_LOW, -4), (C_HIGH, 4), (FAR, 6 * core - 3))
 
-    def attend(g, blocks):
+    def attend(g, blocks, values_here=None):
         query = q_buf[:, columns(g)] * jnp.asarray(HD ** -0.5, jnp.bfloat16)
-        totals, peaks = [], []
-        for half in range(2):
-            mask = lane_head == half
-            chosen = jnp.where(mask, query, jnp.zeros((), jnp.bfloat16))
+        weights, totals, peaks = [], [], []
+        for half in range(2):
+            chosen = jnp.where(lane_head == half, query, jnp.zeros((), jnp.bfloat16))
             slope = slopes[2 * g + half] * LOG2E
             scores = []
             for slot, offset in blocks:
@@ -134,16 +141,21 @@
                 )
                 scores.append(dots * LOG2E + slope * bias[offset + WIN])
             peak = jnp.max(functools.reduce(jnp.maximum, scores), axis=0, keepdims=True)
+            weights.append([jnp.exp2(score - peak).astype(jnp.bfloat16) for score in scores])
+            peaks.append(peak)
+        if values_here is not None:
+            values_here()
+        for half in range(2):
             total = None
-            for score, (slot, _) in zip(scores, blocks):
-                weights = jnp.exp2(score - peak).astype(jnp.bfloat16)
-                value = jnp.where(mask, kv[slot, 1, :, columns(g)], jnp.ones((), jnp.bfloat16))
+            for weight, (slot, _) in zip(weights[half], blocks):
+                value = jnp.where(
+                    lane_head == half, kv[slot, 1, :, columns(g)], jnp.ones((), jnp.bfloat16)
+                )
                 term = lax.dot_general(
-                    value, weights, (((0,), (0,)), ((), ())), preferred_element_type=jnp.float32
+                    value, weight, (((0,), (0,)), ((), ())), preferred_element_type=jnp.float32
                 )
                 total = term if total is None else total + term
             totals.append(total)
-            peaks.append(peak)
         tops = totals[0][:HD], totals[1][HD:]
         lows = totals[0][HD : HD + 1], totals[1][:1]
         return tops, lows, peaks
@@ -179,6 +191,12 @@
             arrived(near_slot[stream], own_chunks, i)
             for j, (inner, _) in enumerate(far_chunks):
                 if start <= inner < start + count:
+                    if j == last:
+                        for part in range(2):
+                            final(
+                                near_slot[stream], far_slot[stream], part, target[stream]
+                            ).start()
+                        continue
                     passing(
                         near_slot[stream], far_slot[stream], far_chunks, j, target[stream]
                     ).start()
@@ -203,14 +221,29 @@
 
     def prepare(j):
         for ahead in shares[j]:
-            share(ahead)
+            if ahead < last:
+                share(ahead)
         arrived(far_slot[1], far_chunks, j)
         arrived(FAR, far_chunks, j)
-
-    @pl.loop(0, groups)
+        if last in shares[j]:
+            share_last()
+
+    def share_last():
+        for part in range(2):
+            final(far_slot[0], far_slot[0], part, sib).wait_recv()
+            final(far_slot[0], FAR, part, sib).start()
+
+    def here(part):
+        final(far_slot[1], far_slot[1], part, sib).wait_recv()
+        final(FAR, FAR, part, sib).wait_recv()
+
+    @pl.loop(0, groups - 1)
     def _(g):
-        at_start(g, far_chunks, prepare)
+        at_start(g, far_chunks[:last], prepare)
         finish(g, attend(g, outer))
+
+    here(0)
+    finish(groups - 1, attend(groups - 1, outer, lambda: here(1)))
 
     for slot in (C_LOW, C_HIGH, FAR):
         left(slot)
@@ -245,7 +278,7 @@
                 pltpu.SMEM(slopes.shape, jnp.float32),
                 pltpu.SemaphoreType.DMA((9,)),
                 pltpu.SemaphoreType.DMA((5, 5)),
-                pltpu.SemaphoreType.DMA((3, 9)),
+                pltpu.SemaphoreType.DMA((3, 10)),
                 pltpu.SemaphoreType.DMA((6,)),
                 pltpu.SemaphoreType.DMA,
             ],

time: 101 us -> 101 us (level)
  no operation moved by 1% of the time
where the time goes in v6:
time: 101 us
  Pallas kernels  99.7 us (99%)
    pallas_call x1, Pallas kernels, per_device(): pl.pallas_call(functools.partial(kernel, ring), out_shape=pltpu.VMEM((row...  99.7 us

profile of v6, /device:TPU:1, one launch (start us, length us, event | category | flops | bytes accessed | tf_op | source)
XLA Modules:
  0.0 100.7 jit_solution(16618907500654475069)
XLA Ops:
  0.0 99.7 %shard_map.64 = bf16[256,2048]{1,0:T(8,128)(2,1)S(1)} custom-call(s32[5]{0:T(128)} %buckets_hbm.1, f32[32]{0:T(128)} %slopes_hbm.1, bf16[256,2048]{1,0:T(8,128)(2,1)} %q_hbm.1, bf16[256,2048]{1,0:T(8,128)(2,1)} %k_hbm.1, bf16[256,2048]{1,0:T(8,128)(2,1)} %v_hbm.1, bf16[3,256,256]{2,1,0:T(8,128)(2,1)} %tiles_hbm.1), custom_call_target="tpu_custom_call" | custom-call | tf_op jit(solution)/shard_map/pallas_call | solution.py:265
  99.7 1.0 copy.8

commit v7 on v6

--- a/solution.py
+++ b/solution.py
@@ -19,7 +19,7 @@
 
 def kernel(
     ring, buckets_hbm, slopes_hbm, q_hbm, k_hbm, v_hbm, tiles_hbm, out_ref,
-    kv, q_buf, tiles, bias, state, sums, buckets, slopes, send_sem, near_sem, far_sem, in_sem, lead_sem,
+    kv, q_buf, tiles, bias, state, sums, buckets, slopes, send_sem, near_sem, far_sem, in_sem, lead_sem, sib_sem,
 ):
     groups = q_buf.shape[1] // LANES
     me = lax.axis_index("seq")
@@ -45,7 +45,7 @@
         )
 
     def recv_sem(slot, chunks, i):
-        return near_sem.at[slot - SIB, i] if chunks is own_chunks else far_sem.at[slot - C_LOW, i]
+        return near_sem.at[slot - A_LOW, i] if chunks is own_chunks else far_sem.at[slot - C_LOW, i]
 
     def send_own(i, slot, device, first_sem=None):
         for part, ref in enumerate((k_hbm, v_hbm)):
@@ -101,8 +101,14 @@
             )
 
     start_stream(0)
-    for i in range(len(own_chunks)):
-        send_own(i, SIB, sib)
+    for part, ref in enumerate((k_hbm, v_hbm)):
+        remote(ref, kv.at[SIB, part], send_sem.at[SIB], sib_sem, sib).start()
+
+    head = columns(*own_chunks[0])
+    remote(
+        k_hbm.at[:, head], kv.at[OWN, 0, :, head], lead_sem, near_sem.at[0, 0], sib
+    ).wait_send()
+    start_stream(1)
 
     loads[0].wait()
     loads[1].wait()
@@ -112,11 +118,6 @@
         if o > 0:
             bias[WIN - o] = tile
 
-    head = columns(*own_chunks[0])
-    remote(
-        k_hbm.at[:, head], kv.at[OWN, 0, :, head], lead_sem, near_sem.at[0, 0], sib
-    ).wait_send()
-    start_stream(1)
     for load in loads[2:]:
         load.wait()
 
@@ -201,8 +202,10 @@
                         near_slot[stream], far_slot[stream], far_chunks, j, target[stream]
                     ).start()
             passing(near_slot[stream], sib_slot[stream], own_chunks, i, sib).start()
-        for slot in (SIB, B_LOW, B_HIGH):
+        for slot in (B_LOW, B_HIGH):
             arrived(slot, own_chunks, i)
+        if i == 0:
+            remote(kv.at[SIB], kv.at[SIB], send_sem.at[SIB], sib_sem, sib).wait_recv()
 
     @pl.loop(0, groups)
     def _(g):
@@ -277,9 +280,10 @@
                 pltpu.SMEM(buckets.shape, jnp.int32),
                 pltpu.SMEM(slopes.shape, jnp.float32),
                 pltpu.SemaphoreType.DMA((9,)),
-                pltpu.SemaphoreType.DMA((5, 5)),
+                pltpu.SemaphoreType.DMA((4, 5)),
                 pltpu.SemaphoreType.DMA((3, 10)),
                 pltpu.SemaphoreType.DMA((6,)),
+                pltpu.SemaphoreType.DMA,
                 pltpu.SemaphoreType.DMA,
             ],
             compiler_params=pltpu.CompilerParams(

time: 101 us -> 101 us (level)
  no operation moved by 1% of the time
where the time goes in v7:
time: 101 us
  Pallas kernels  99.7 us (99%)
    pallas_call x1, Pallas kernels, per_device(): pl.pallas_call(functools.partial(kernel, ring), out_shape=pltpu.VMEM((row...  99.7 us

profile of v7, /device:TPU:1, one launch (start us, length us, event | category | flops | bytes accessed | tf_op | source)
XLA Modules:
  0.0 100.7 jit_solution(12900528478189480732)
XLA Ops:
  0.0 99.7 %shard_map.64 = bf16[256,2048]{1,0:T(8,128)(2,1)S(1)} custom-call(s32[5]{0:T(128)} %buckets_hbm.1, f32[32]{0:T(128)} %slopes_hbm.1, bf16[256,2048]{1,0:T(8,128)(2,1)} %q_hbm.1, bf16[256,2048]{1,0:T(8,128)(2,1)} %k_hbm.1, bf16[256,2048]{1,0:T(8,128)(2,1)} %v_hbm.1, bf16[3,256,256]{2,1,0:T(8,128)(2,1)} %tiles_hbm.1), custom_call_target="tpu_custom_call" | custom-call | tf_op jit(solution)/shard_map/pallas_call | solution.py:268
  99.7 1.0 copy.8
